TPU v7x, 256 devices: a whole 4x4x8 slice. The times are simulated.
256 devices in a mesh: expert: 8 (over y_lo, x), fsdp: 32 (over y_hi, z, core).
Axes of the slice: x: 4, y: 4 (y_hi: 2, y_lo: 2; y = y_hi * 2 + y_lo), z: 8, core: 2. Of those that a mesh axis runs over, the one named last changes fastest.
Arguments:
- tokens: bfloat16 [1024, 3072], P('expert'), may hold values from -6 to 6
- assignment: int32 [1024, 2], P('expert'), may hold values from 0 to 7, all different within a row; in each aligned block of 128 rows (0 to 127, 128 to 255, ...) at most 48 rows name the same one
- route_weight: float32 [1024, 2], P('expert'), may hold values from 0.25 to 1
- cotangent: bfloat16 [1024, 3072], P('expert'), may hold values from -6 to 6
- w_gate: bfloat16 [8, 3072, 8192], P('expert', None, 'fsdp'), may hold values from -0.109375 to 0.109375
- w_up: bfloat16 [8, 3072, 8192], P('expert', None, 'fsdp'), may hold values from -0.109375 to 0.109375
- w_down: bfloat16 [8, 8192, 3072], P('expert', 'fsdp'), may hold values from -0.0625 to 0.0625
Outputs:
- moe_out: bfloat16 [1024, 3072], P('expert')
- grad_tokens: bfloat16 [1024, 3072], P('expert')
- grad_prob: float32 [1024, 2], P('expert')
- grad_gate: bfloat16 [8, 3072, 8192], P('expert', None, 'fsdp')
- grad_up: bfloat16 [8, 3072, 8192], P('expert', None, 'fsdp')
- grad_down: bfloat16 [8, 8192, 3072], P('expert', 'fsdp')
Inputs may be any that keep to these rules, and one draw needn't show every extreme that they name: `assignment`: each token names two different experts. Among the 128 tokens of one block no expert is named more than 48 times, and in some block some expert is named exactly 48 times.
All inputs are finite; a program needn't handle non-finite values.
Results may differ from a plain program's by a relative error of at most 0.02.
Values may be sent and summed in bfloat16 or wider, within the bound.
A program may use at most 128 MiB of HBM per device.

v0:
```python
import jax
import jax.numpy as jnp
from jax import lax
from jax.sharding import PartitionSpec as P


def slot_table(assignment, groups, capacity):
    flat = assignment.reshape(-1)
    onehot = (flat[:, None] == jnp.arange(groups, dtype=jnp.int32)[None, :]).astype(jnp.int32)
    before = jnp.cumsum(onehot, axis=0) - onehot
    position = jnp.sum(before * onehot, axis=1)
    return (flat * capacity + position).reshape(assignment.shape)


def front_half(gathered, gate_local, up_local):
    pre_gate = jnp.dot(gathered, gate_local, preferred_element_type=jnp.float32)
    pre_up = jnp.dot(gathered, up_local, preferred_element_type=jnp.float32)
    sigma = jax.nn.sigmoid(pre_gate)
    silu_gate = pre_gate * sigma
    hidden = (silu_gate * pre_up).astype(jnp.bfloat16)
    return (pre_gate, pre_up, sigma, silu_gate, hidden)


def spread(buffer, groups, capacity):
    width = buffer.shape[-1]
    blocks = buffer.reshape(groups, capacity, width)
    arrived = lax.all_to_all(blocks, "expert", split_axis=0, concat_axis=0, tiled=True)
    return arrived.reshape(-1, width)


def return_rows(term_fn, rows, groups, capacity, width):
    shares = lax.psum_scatter(
        term_fn(jnp.int32(0), rows * lax.axis_size("fsdp")).astype(jnp.bfloat16),
        "fsdp",
        scatter_dimension=0,
        tiled=True,
    )
    summed = lax.all_gather(shares, "fsdp", axis=0, tiled=True)
    back = lax.all_to_all(
        summed.reshape(groups, capacity, width), "expert", split_axis=0, concat_axis=0, tiled=True
    )
    return back.reshape(-1, width)


def per_device(tokens, assignment, route_weight, cotangent, w_gate, w_up, w_down):
    tok_dev = tokens.shape[0]
    width = tokens.shape[1]
    groups = lax.axis_size("expert")
    capacity = max(2, 3 * tok_dev // groups)
    slot_count = groups * capacity
    share_rows = slot_count // lax.axis_size("fsdp")
    table = slot_table(assignment, groups, capacity)
    slot_ids = jnp.arange(slot_count, dtype=jnp.int32)
    pick_first = slot_ids[:, None] == table[:, 0][None, :]
    pick_second = slot_ids[:, None] == table[:, 1][None, :]
    pick_both = jnp.logical_or(pick_first, pick_second).astype(jnp.bfloat16)
    sent_tokens = jnp.dot(pick_both, tokens, preferred_element_type=jnp.float32).astype(
        jnp.bfloat16
    )
    weighted = (route_weight[:, :, None] * cotangent[:, None, :].astype(jnp.float32)).astype(
        jnp.bfloat16
    )
    sent_cot = (
        jnp.dot(pick_first.astype(jnp.bfloat16), weighted[:, 0], preferred_element_type=jnp.float32)
        + jnp.dot(
            pick_second.astype(jnp.bfloat16), weighted[:, 1], preferred_element_type=jnp.float32
        )
    ).astype(jnp.bfloat16)
    gate_local = w_gate[0]
    up_local = w_up[0]
    down_local = w_down[0]
    gathered = spread(sent_tokens, groups, capacity)
    pre_gate, pre_up, sigma, silu_gate, hidden = front_half(gathered, gate_local, up_local)

    def out_term(start, count):
        return jnp.dot(hidden, down_local, preferred_element_type=jnp.float32)

    out_back = return_rows(out_term, share_rows, groups, capacity, width).astype(jnp.float32)
    select_first = pick_first.astype(jnp.float32)
    select_second = pick_second.astype(jnp.float32)
    first_out = jnp.dot(select_first.T, out_back, precision=lax.Precision.HIGHEST)
    second_out = jnp.dot(select_second.T, out_back, precision=lax.Precision.HIGHEST)
    moe_out = (route_weight[:, 0:1] * first_out + route_weight[:, 1:2] * second_out).astype(
        jnp.bfloat16
    )
    cot_float = cotangent.astype(jnp.float32)
    grad_prob = jnp.stack(
        [jnp.sum(cot_float * first_out, axis=1), jnp.sum(cot_float * second_out, axis=1)], axis=1
    )
    grad_gathered = spread(sent_cot, groups, capacity)
    grad_hidden = jnp.dot(grad_gathered, down_local.T, preferred_element_type=jnp.float32)
    grad_down = jnp.dot(hidden.T, grad_gathered, preferred_element_type=jnp.float32).astype(
        jnp.bfloat16
    )
    grad_pre_gate = (grad_hidden * pre_up * sigma * (1.0 + pre_gate * (1.0 - sigma))).astype(
        jnp.bfloat16
    )
    grad_pre_up = (grad_hidden * silu_gate).astype(jnp.bfloat16)
    grad_gate = jnp.dot(gathered.T, grad_pre_gate, preferred_element_type=jnp.float32).astype(
        jnp.bfloat16
    )
    grad_up = jnp.dot(gathered.T, grad_pre_up, preferred_element_type=jnp.float32).astype(
        jnp.bfloat16
    )

    def back_term(start, count):
        return jnp.dot(grad_pre_gate, gate_local.T, preferred_element_type=jnp.float32) + jnp.dot(
            grad_pre_up, up_local.T, preferred_element_type=jnp.float32
        )

    grad_back = return_rows(back_term, share_rows, groups, capacity, width).astype(jnp.float32)
    grad_tokens = (
        jnp.dot(select_first.T, grad_back, precision=lax.Precision.HIGHEST)
        + jnp.dot(select_second.T, grad_back, precision=lax.Precision.HIGHEST)
    ).astype(jnp.bfloat16)
    return (moe_out, grad_tokens, grad_prob, grad_gate[None], grad_up[None], grad_down[None])


def solution(mesh):
    return jax.shard_map(
        per_device,
        mesh=mesh,
        in_specs=(
            P("expert", None),
            P("expert", None),
            P("expert", None),
            P("expert", None),
            P("expert", None, "fsdp"),
            P("expert", None, "fsdp"),
            P("expert", "fsdp", None),
        ),
        out_specs=(
            P("expert", None),
            P("expert", None),
            P("expert", None),
            P("expert", None, "fsdp"),
            P("expert", None, "fsdp"),
            P("expert", "fsdp", None),
        ),
        check_vma=False,
    )
```

profile of v0, /device:TPU:6, one launch (start us, length us, event | category | flops | bytes accessed | tf_op | source)
XLA Modules:
  0.0 465.9 jit_solution(11138213794973551333)
XLA Ops:
  13.6 6.6 %all-to-all-start = ((bf16[8,48,3072]{2,1,0:T(8,128)(2,1)}), bf16[8,48,3072]{2,1,0:T(8,128)(2,1)}, u32[]{:S(2)}, u32[]{:S(2)}) async-start(bf16[8,48,3072]{2,1,0:T(8,128)(2,1)} %bitcast.80), calls=%async_computation | async-start | bytes 4718592 | tf_op jit(solution)/shard_map/all_to_all | solution.py:27
  23.6 25.5 %all-to-all-done = bf16[8,48,3072]{2,1,0:T(8,128)(2,1)} async-done(((bf16[8,48,3072]{2,1,0:T(8,128)(2,1)}), bf16[8,48,3072]{2,1,0:T(8,128)(2,1)}, u32[]{:S(2)}, u32[]{:S(2)}) %all-to-all-start) | async-done | bytes 2359328 | tf_op jit(solution)/shard_map/all_to_all | solution.py:27
  49.1 5.4 %all-to-all-start.2 = ((bf16[8,48,3072]{2,1,0:T(8,128)(2,1)}), bf16[8,48,3072]{2,1,0:T(8,128)(2,1)}, u32[]{:S(2)}, u32[]{:S(2)}) async-start(bf16[8,48,3072]{2,1,0:T(8,128)(2,1)} %bitcast.81), calls=%async_computation.2 | async-start | bytes 4718592 | tf_op jit(solution)/shard_map/all_to_all | solution.py:27
  61.5 21.2 %all-to-all-done.2 = bf16[8,48,3072]{2,1,0:T(8,128)(2,1)} async-done(((bf16[8,48,3072]{2,1,0:T(8,128)(2,1)}), bf16[8,48,3072]{2,1,0:T(8,128)(2,1)}, u32[]{:S(2)}, u32[]{:S(2)}) %all-to-all-start.2) | async-done | bytes 2359328 | tf_op jit(solution)/shard_map/all_to_all | solution.py:27
  90.8 86.6 %fusion.34 = (bf16[16,3072]{1,0:T(8,128)(2,1)S(1)}, bf16[16,3072]{1,0:T(8,128)(2,1)S(1)}) fusion(bf16[384,3072]{1,0:T(8,128)(2,1)} %convolution_convert_fusion.1, bf16[384,3072]{1,0:T(8,128)(2,1)} %add_convert_fusion), kind=kCustom, calls=%all-reduce-scatter.2 | all-reduce-scatter fusion | flops 3145729 | bytes 4916224
  182.7 10.9 %collective-permute-start.3 = (bf16[16,3072]{1,0:T(8,128)(2,1)S(1)}, bf16[16,3072]{1,0:T(8,128)(2,1)S(1)}, u32[]{:S(2)}, u32[]{:S(2)}) collective-permute-start(bf16[16,3072]{1,0:T(8,128)(2,1)S(1)} %get-tuple-element.10), channel_id=1, source_target_pairs={{0,4},{1,5},{2,6},{3,7},{4,8},{5,9},{6,10},{7,11},{8,12},{9,13},{1... | collective-permute-start | bytes 294920
  198.1 5.3 %collective-permute-start.6 = (bf16[16,3072]{1,0:T(8,128)(2,1)S(1)}, bf16[16,3072]{1,0:T(8,128)(2,1)}, u32[]{:S(2)}, u32[]{:S(2)}) collective-permute-start(bf16[16,3072]{1,0:T(8,128)(2,1)S(1)} %get-tuple-element.10), channel_id=1, source_target_pairs={{0,7},{1,8},{2,9},{3,10},{4,11},{5,12},{6,13},{7,14},{8,15},{9,16}... | collective-permute-start | bytes 294920
  204.7 4.6 collective-permute-done.5
  209.9 4.3 collective-permute-done.6
  214.2 6.5 %concatenate = bf16[140,3072]{1,0:T(8,128)(2,1)S(1)} concatenate(bf16[12,3072]{1,0:T(8,128)(2,1)S(1)} %collective-permute-done.7, bf16[16,3072]{1,0:T(8,128)(2,1)} %collective-permute-done.6, bf16[16,3072]{1,0:T(8,128)(2,1)} %copy-done.8, bf16[16,3072]{1,0:T(8,128)(2,1)} %copy-done.7, bf16[16,3072]{1,0:T(8,128)(2,1)S(1)} %collective-permute-done.3, ...), dimensions={0} | concatenate | bytes 1720320
  222.8 6.9 %collective-permute-start.11 = (bf16[16,3072]{1,0:T(8,128)(2,1)S(1)}, bf16[16,3072]{1,0:T(8,128)(2,1)S(1)}, u32[]{:S(2)}, u32[]{:S(2)}) collective-permute-start(bf16[16,3072]{1,0:T(8,128)(2,1)S(1)} %get-tuple-element.11), channel_id=1, source_target_pairs={{0,4},{1,5},{2,6},{3,7},{4,8},{5,9},{6,10},{7,11},{8,12},{9,13},{1... | collective-permute-start | bytes 294920
  229.7 4.3 collective-permute-start.15
  234.0 7.4 %collective-permute-start.12 = (bf16[16,3072]{1,0:T(8,128)(2,1)S(1)}, bf16[16,3072]{1,0:T(8,128)(2,1)S(1)}, u32[]{:S(2)}, u32[]{:S(2)}) collective-permute-start(bf16[16,3072]{1,0:T(8,128)(2,1)S(1)} %get-tuple-element.11), channel_id=1, source_target_pairs={{0,5},{1,6},{2,7},{3,8},{4,9},{5,10},{6,11},{7,12},{8,13},{9,14},{... | collective-permute-start | bytes 294920
  247.6 6.7 %collective-permute-start.9 = (bf16[16,3072]{1,0:T(8,128)(2,1)S(1)}, bf16[16,3072]{1,0:T(8,128)(2,1)}, u32[]{:S(2)}, u32[]{:S(2)}) collective-permute-start(bf16[16,3072]{1,0:T(8,128)(2,1)S(1)} %get-tuple-element.11), channel_id=1, source_target_pairs={{0,2},{1,3},{2,4},{3,5},{4,6},{5,7},{6,8},{7,9},{8,10},{9,11},{10,... | collective-permute-start | bytes 294920
  264.3 5.1 %concatenate.1 = bf16[140,3072]{1,0:T(8,128)(2,1)S(1)} concatenate(bf16[12,3072]{1,0:T(8,128)(2,1)S(1)} %collective-permute-done.15, bf16[16,3072]{1,0:T(8,128)(2,1)S(1)} %collective-permute-done.14, bf16[16,3072]{1,0:T(8,128)(2,1)S(1)} %collective-permute-done.13, bf16[16,3072]{1,0:T(8,128)(2,1)S(1)} %collective-permute-done.12, bf16[16,3072]{1,0:T(8,128)(2,1)S(1)} %collective-permute-done.11, ...), dimensions={0} | concatenate | bytes 1720320
  270.1 39.0 %all-gather.5.cloned.1.call-done = bf16[32,12,3072]{2,1,0:T(8,128)(2,1)} async-done(((bf16[1,12,3072]{2,1,0:T(8,128)(2,1)}), bf16[32,12,3072]{2,1,0:T(8,128)(2,1)}) %all-gather.5.cloned.1.call-update) | async-done | bytes 2359312 | tf_op jit(solution)/shard_map/all_gather | solution.py:38
  309.0 4.3 reshape.64
  313.3 4.8 %all-to-all-start.1 = ((bf16[8,48,3072]{2,1,0:T(8,128)(2,1)}), bf16[8,48,3072]{2,1,0:T(8,128)(2,1)}, u32[]{:S(2)}, u32[]{:S(2)}) async-start(bf16[8,48,3072]{2,1,0:T(8,128)(2,1)} %reshape.64), calls=%async_computation.1 | async-start | bytes 4718592 | tf_op jit(solution)/shard_map/all_to_all | solution.py:39
  318.1 87.1 %all-gather.7.cloned.1.call-done = bf16[32,12,3072]{2,1,0:T(8,128)(2,1)} async-done(((bf16[1,12,3072]{2,1,0:T(8,128)(2,1)}), bf16[32,12,3072]{2,1,0:T(8,128)(2,1)}) %all-gather.7.cloned.1.call-update) | async-done | bytes 2359312 | tf_op jit(solution)/shard_map/all_gather | solution.py:38
  405.3 4.2 reshape.68
  409.5 4.8 %all-to-all-start.3 = ((bf16[8,48,3072]{2,1,0:T(8,128)(2,1)}), bf16[8,48,3072]{2,1,0:T(8,128)(2,1)}, u32[]{:S(2)}, u32[]{:S(2)}) async-start(bf16[8,48,3072]{2,1,0:T(8,128)(2,1)} %reshape.68), calls=%async_computation.3 | async-start | bytes 4718592 | tf_op jit(solution)/shard_map/all_to_all | solution.py:39
  418.7 3.9 fusion.2
  422.5 3.8 fusion.3
  428.7 20.8 %all-to-all-done.3 = bf16[8,48,3072]{2,1,0:T(8,128)(2,1)} async-done(((bf16[8,48,3072]{2,1,0:T(8,128)(2,1)}), bf16[8,48,3072]{2,1,0:T(8,128)(2,1)}, u32[]{:S(2)}, u32[]{:S(2)}) %all-to-all-start.3) | async-done | bytes 2359328 | tf_op jit(solution)/shard_map/all_to_all | solution.py:39
  (91 shorter events, 70.9 us)
Async XLA Ops:
  7.2 75.6 %copy-start = (bf16[1,256,3072]{2,1,0:T(8,128)(2,1)S(1)}, bf16[1,256,3072]{2,1,0:T(8,128)(2,1)}, u32[]{:S(2)}) copy-start(bf16[1,256,3072]{2,1,0:T(8,128)(2,1)} %param.13) | copy-start | bytes 4718596
  13.6 35.6 %all-to-all-start = ((bf16[8,48,3072]{2,1,0:T(8,128)(2,1)}), bf16[8,48,3072]{2,1,0:T(8,128)(2,1)}, u32[]{:S(2)}, u32[]{:S(2)}) async-start(bf16[8,48,3072]{2,1,0:T(8,128)(2,1)} %bitcast.80), calls=%async_computation | async-start | bytes 4718592 | tf_op jit(solution)/shard_map/all_to_all | solution.py:27
  49.1 33.6 %all-to-all-start.2 = ((bf16[8,48,3072]{2,1,0:T(8,128)(2,1)}), bf16[8,48,3072]{2,1,0:T(8,128)(2,1)}, u32[]{:S(2)}, u32[]{:S(2)}) async-start(bf16[8,48,3072]{2,1,0:T(8,128)(2,1)} %bitcast.81), calls=%async_computation.2 | async-start | bytes 4718592 | tf_op jit(solution)/shard_map/all_to_all | solution.py:27
  54.6 254.5 %all-gather.5.cloned.1.call-start = ((), (), s32[]{:S(2)}) async-start(), calls=%async_computation.4 | async-start | bytes 3244032 | tf_op jit(solution)/shard_map/all_gather | solution.py:38
  90.8 112.6 %copy-start.12 = (u32[256]{0:T(256)S(1)}, u32[256]{0:T(256)}, u32[]{:S(2)}) copy-start(u32[256]{0:T(256)} %constant.17) | copy-start | bytes 3076
  177.4 17.9 %collective-permute-start = (bf16[16,3072]{1,0:T(8,128)(2,1)S(1)}, bf16[16,3072]{1,0:T(8,128)(2,1)S(1)}, u32[]{:S(2)}, u32[]{:S(2)}) collective-permute-start(bf16[16,3072]{1,0:T(8,128)(2,1)S(1)} %get-tuple-element.10), channel_id=1, source_target_pairs={{0,1},{1,2},{2,3},{3,4},{4,5},{5,6},{6,7},{7,8},{8,9},{9,10},{10,1... | collective-permute-start | bytes 294920
  178.7 19.3 %collective-permute-start.1 = (bf16[16,3072]{1,0:T(8,128)(2,1)S(1)}, bf16[16,3072]{1,0:T(8,128)(2,1)S(1)}, u32[]{:S(2)}, u32[]{:S(2)}) collective-permute-start(bf16[16,3072]{1,0:T(8,128)(2,1)S(1)} %get-tuple-element.10), channel_id=1, source_target_pairs={{0,2},{1,3},{2,4},{3,5},{4,6},{5,7},{6,8},{7,9},{8,10},{9,11},{10,... | collective-permute-start | bytes 294920
  180.1 13.6 %collective-permute-start.7 = (bf16[12,3072]{1,0:T(8,128)(2,1)S(1)}, bf16[12,3072]{1,0:T(8,128)(2,1)S(1)}, u32[]{:S(2)}, u32[]{:S(2)}) collective-permute-start(bf16[12,3072]{1,0:T(8,128)(2,1)S(1)} %slice.35), channel_id=1, source_target_pairs={{0,8},{1,9},{2,10},{3,11},{4,12},{5,13},{6,14},{7,15},{8,16},{9,17... | collective-permute-start | bytes 221192
  181.4 23.3 %collective-permute-start.2 = (bf16[16,3072]{1,0:T(8,128)(2,1)S(1)}, bf16[16,3072]{1,0:T(8,128)(2,1)S(1)}, u32[]{:S(2)}, u32[]{:S(2)}) collective-permute-start(bf16[16,3072]{1,0:T(8,128)(2,1)S(1)} %get-tuple-element.10), channel_id=1, source_target_pairs={{0,3},{1,4},{2,5},{3,6},{4,7},{5,8},{6,9},{7,10},{8,11},{9,12},{10... | collective-permute-start | bytes 294920
  182.7 22.0 %collective-permute-start.3 = (bf16[16,3072]{1,0:T(8,128)(2,1)S(1)}, bf16[16,3072]{1,0:T(8,128)(2,1)S(1)}, u32[]{:S(2)}, u32[]{:S(2)}) collective-permute-start(bf16[16,3072]{1,0:T(8,128)(2,1)S(1)} %get-tuple-element.10), channel_id=1, source_target_pairs={{0,4},{1,5},{2,6},{3,7},{4,8},{5,9},{6,10},{7,11},{8,12},{9,13},{1... | collective-permute-start | bytes 294920
  193.6 11.0 %collective-permute-start.4 = (bf16[16,3072]{1,0:T(8,128)(2,1)S(1)}, bf16[16,3072]{1,0:T(8,128)(2,1)S(1)}, u32[]{:S(2)}, u32[]{:S(2)}) collective-permute-start(bf16[16,3072]{1,0:T(8,128)(2,1)S(1)} %get-tuple-element.10), channel_id=1, source_target_pairs={{0,5},{1,6},{2,7},{3,8},{4,9},{5,10},{6,11},{7,12},{8,13},{9,14},{... | collective-permute-start | bytes 294920
  195.3 13.9 %collective-permute-start.5 = (bf16[16,3072]{1,0:T(8,128)(2,1)S(1)}, bf16[16,3072]{1,0:T(8,128)(2,1)S(1)}, u32[]{:S(2)}, u32[]{:S(2)}) collective-permute-start(bf16[16,3072]{1,0:T(8,128)(2,1)S(1)} %get-tuple-element.10), channel_id=1, source_target_pairs={{0,6},{1,7},{2,8},{3,9},{4,10},{5,11},{6,12},{7,13},{8,14},{9,15},... | collective-permute-start | bytes 294920
  198.1 16.1 %collective-permute-start.6 = (bf16[16,3072]{1,0:T(8,128)(2,1)S(1)}, bf16[16,3072]{1,0:T(8,128)(2,1)}, u32[]{:S(2)}, u32[]{:S(2)}) collective-permute-start(bf16[16,3072]{1,0:T(8,128)(2,1)S(1)} %get-tuple-element.10), channel_id=1, source_target_pairs={{0,7},{1,8},{2,9},{3,10},{4,11},{5,12},{6,13},{7,14},{8,15},{9,16}... | collective-permute-start | bytes 294920
  221.4 183.9 %all-gather.7.cloned.1.call-start = ((), (), s32[]{:S(2)}) async-start(), calls=%async_computation.5 | async-start | bytes 3244032 | tf_op jit(solution)/shard_map/all_gather | solution.py:38
  221.5 24.1 %collective-permute-start.10 = (bf16[16,3072]{1,0:T(8,128)(2,1)S(1)}, bf16[16,3072]{1,0:T(8,128)(2,1)S(1)}, u32[]{:S(2)}, u32[]{:S(2)}) collective-permute-start(bf16[16,3072]{1,0:T(8,128)(2,1)S(1)} %get-tuple-element.11), channel_id=1, source_target_pairs={{0,3},{1,4},{2,5},{3,6},{4,7},{5,8},{6,9},{7,10},{8,11},{9,12},{10... | collective-permute-start | bytes 294920
  222.8 24.8 %collective-permute-start.11 = (bf16[16,3072]{1,0:T(8,128)(2,1)S(1)}, bf16[16,3072]{1,0:T(8,128)(2,1)S(1)}, u32[]{:S(2)}, u32[]{:S(2)}) collective-permute-start(bf16[16,3072]{1,0:T(8,128)(2,1)S(1)} %get-tuple-element.11), channel_id=1, source_target_pairs={{0,4},{1,5},{2,6},{3,7},{4,8},{5,9},{6,10},{7,11},{8,12},{9,13},{1... | collective-permute-start | bytes 294920
  229.7 13.0 %collective-permute-start.15 = (bf16[12,3072]{1,0:T(8,128)(2,1)S(1)}, bf16[12,3072]{1,0:T(8,128)(2,1)S(1)}, u32[]{:S(2)}, u32[]{:S(2)}) collective-permute-start(bf16[12,3072]{1,0:T(8,128)(2,1)S(1)} %slice.36), channel_id=1, source_target_pairs={{0,8},{1,9},{2,10},{3,11},{4,12},{5,13},{6,14},{7,15},{8,16},{9,17... | collective-permute-start | bytes 221192
  234.0 20.3 %collective-permute-start.12 = (bf16[16,3072]{1,0:T(8,128)(2,1)S(1)}, bf16[16,3072]{1,0:T(8,128)(2,1)S(1)}, u32[]{:S(2)}, u32[]{:S(2)}) collective-permute-start(bf16[16,3072]{1,0:T(8,128)(2,1)S(1)} %get-tuple-element.11), channel_id=1, source_target_pairs={{0,5},{1,6},{2,7},{3,8},{4,9},{5,10},{6,11},{7,12},{8,13},{9,14},{... | collective-permute-start | bytes 294920
  241.4 16.4 %collective-permute-start.13 = (bf16[16,3072]{1,0:T(8,128)(2,1)S(1)}, bf16[16,3072]{1,0:T(8,128)(2,1)S(1)}, u32[]{:S(2)}, u32[]{:S(2)}) collective-permute-start(bf16[16,3072]{1,0:T(8,128)(2,1)S(1)} %get-tuple-element.11), channel_id=1, source_target_pairs={{0,6},{1,7},{2,8},{3,9},{4,10},{5,11},{6,12},{7,13},{8,14},{9,15},... | collective-permute-start | bytes 294920
  242.7 18.3 %collective-permute-start.14 = (bf16[16,3072]{1,0:T(8,128)(2,1)S(1)}, bf16[16,3072]{1,0:T(8,128)(2,1)S(1)}, u32[]{:S(2)}, u32[]{:S(2)}) collective-permute-start(bf16[16,3072]{1,0:T(8,128)(2,1)S(1)} %get-tuple-element.11), channel_id=1, source_target_pairs={{0,7},{1,8},{2,9},{3,10},{4,11},{5,12},{6,13},{7,14},{8,15},{9,16}... | collective-permute-start | bytes 294920
  245.5 15.5 %collective-permute-start.8 = (bf16[16,3072]{1,0:T(8,128)(2,1)S(1)}, bf16[16,3072]{1,0:T(8,128)(2,1)S(1)}, u32[]{:S(2)}, u32[]{:S(2)}) collective-permute-start(bf16[16,3072]{1,0:T(8,128)(2,1)S(1)} %get-tuple-element.11), channel_id=1, source_target_pairs={{0,1},{1,2},{2,3},{3,4},{4,5},{5,6},{6,7},{7,8},{8,9},{9,10},{10,1... | collective-permute-start | bytes 294920
  247.6 16.7 %collective-permute-start.9 = (bf16[16,3072]{1,0:T(8,128)(2,1)S(1)}, bf16[16,3072]{1,0:T(8,128)(2,1)}, u32[]{:S(2)}, u32[]{:S(2)}) collective-permute-start(bf16[16,3072]{1,0:T(8,128)(2,1)S(1)} %get-tuple-element.11), channel_id=1, source_target_pairs={{0,2},{1,3},{2,4},{3,5},{4,6},{5,7},{6,8},{7,9},{8,10},{9,11},{10,... | collective-permute-start | bytes 294920
  313.3 96.2 %all-to-all-start.1 = ((bf16[8,48,3072]{2,1,0:T(8,128)(2,1)}), bf16[8,48,3072]{2,1,0:T(8,128)(2,1)}, u32[]{:S(2)}, u32[]{:S(2)}) async-start(bf16[8,48,3072]{2,1,0:T(8,128)(2,1)} %reshape.64), calls=%async_computation.1 | async-start | bytes 4718592 | tf_op jit(solution)/shard_map/all_to_all | solution.py:39
  409.5 39.9 %all-to-all-start.3 = ((bf16[8,48,3072]{2,1,0:T(8,128)(2,1)}), bf16[8,48,3072]{2,1,0:T(8,128)(2,1)}, u32[]{:S(2)}, u32[]{:S(2)}) async-start(bf16[8,48,3072]{2,1,0:T(8,128)(2,1)} %reshape.68), calls=%async_computation.3 | async-start | bytes 4718592 | tf_op jit(solution)/shard_map/all_to_all | solution.py:39
  (11 other events, 38.7 us)
Sparse Core Ops, SparseCore 0:
  221.5 87.4 all-gather.4
  312.4 92.8 all-gather.6
where the time goes:
time: 468 us; the launch traced here: 466 us
  waiting for transfers between devices  212 us (45%)
  blocking collectives  86.6 us (19%)
  starting transfers between devices  80.2 us (17%)
  matrix products  44.2 us (9%)
  local copies, waits for them, and re-layouts  25.5 us (5%)
  between operations  15.1 us (3%)
    all_gather x2, waiting for transfers between devices, return_rows(): summed = lax.all_gather(shares, 'fsdp', axis=0, tiled=True)  126 us
    unnamed x1, blocking collectives  86.6 us
    unnamed x16, starting transfers between devices  58.5 us
    all_to_all x2, waiting for transfers between devices, spread(): lax.all_to_all(blocks, 'expert', split_axis=0, concat_axis=0, tiled=True)  46.7 us
    all_to_all x2, waiting for transfers between devices, return_rows(): lax.all_to_all(summed.reshape(groups, capacity, width), 'expert', split_a...  20.8 us
    unnamed x18, waiting for transfers between devices  18.3 us
    unnamed x34, local copies, waits for them, and re-layouts  15.8 us
    all_to_all x2, starting transfers between devices, spread(): lax.all_to_all(blocks, 'expert', split_axis=0, concat_axis=0, tiled=True)  12 us
  transfers between devices with their start and end apart: 22, of which 10 were waited for; matrix products, arithmetic and copies ran while one was open for 8% of the time, Pallas kernels for 0%

commit v1 on v0

--- a/solution.py
+++ b/solution.py
@@ -35,7 +35,9 @@
         scatter_dimension=0,
         tiled=True,
     )
-    summed = lax.all_gather(shares, "fsdp", axis=0, tiled=True)
+    summed = jnp.concatenate(
+        lax.all_to_all(jnp.stack([shares] * lax.axis_size("fsdp")), "fsdp", 0, 0), axis=0
+    )
     back = lax.all_to_all(
         summed.reshape(groups, capacity, width), "expert", split_axis=0, concat_axis=0, tiled=True
     )

time: 468 us -> 515 us (1.10)
  starting transfers between devices: 80.2 us -> 111 us
  waiting for transfers between devices: 212 us -> 230 us
  between operations: 15.1 us -> 1.74 us
  local copies, waits for them, and re-layouts: 25.5 us -> 37.8 us
    all_gather x2 -> x0, waiting for transfers between devices: 126 us -> none  [return_rows(): summed = lax.all_gather(shares, 'fsdp', axis=0, tiled=True)]
    all_to_all x0 -> x2, waiting for transfers between devices: none -> 72.1 us  [return_rows(): lax.all_to_all(jnp.stack([shares] * lax.axis_size('fsdp')), 'fsdp', 0, 0)]
    unnamed x18 -> x16, waiting for transfers between devices: 18.3 us -> 68.6 us
    all_to_all x0 -> x2, starting transfers between devices: none -> 24.8 us  [return_rows(): lax.all_to_all(jnp.stack([shares] * lax.axis_size('fsdp')), 'fsdp', 0, 0)]
    all_to_all x2, waiting for transfers between devices: 20.8 us -> 41.7 us  [return_rows(): lax.all_to_all(summed.reshape(groups, capacity, width), 'expert', split_a...]
    unnamed x34 -> x52, local copies, waits for them, and re-layouts: 15.8 us -> 26.6 us
    another operation x1 -> x5, local copies, waits for them, and re-layouts: 0.01 us -> 10.5 us  [the longest x2 6.41 us: return_rows(): summed.reshape(groups, capacity, width)]
    reshape x2 -> x0, local copies, waits for them, and re-layouts: 8.5 us -> none  [return_rows(): summed.reshape(groups, capacity, width)]
  transfers between devices with their start and end apart: 22 -> 22, of which waited for: 10 -> 10; matrix products, arithmetic and copies ran while one was open for 8% -> 10% of each run, Pallas kernels for 0% -> 0%
where the time goes in v1:
time: 515 us; the launch traced here: 511 us
  waiting for transfers between devices  230 us (45%)
  starting transfers between devices  111 us (22%)
  blocking collectives  86 us (17%)
  matrix products  42.1 us (8%)
  local copies, waits for them, and re-layouts  37.8 us (7%)
    unnamed x1, blocking collectives  86 us
    all_to_all x2, waiting for transfers between devices, return_rows(): lax.all_to_all(jnp.stack([shares] * lax.axis_size('fsdp')), 'fsdp', 0, 0)  72.1 us
    unnamed x16, waiting for transfers between devices  68.6 us
    unnamed x16, starting transfers between devices  62.7 us
    all_to_all x2, waiting for transfers between devices, spread(): lax.all_to_all(blocks, 'expert', split_axis=0, concat_axis=0, tiled=True)  47.4 us
    all_to_all x2, waiting for transfers between devices, return_rows(): lax.all_to_all(summed.reshape(groups, capacity, width), 'expert', split_a...  41.7 us
    unnamed x52, local copies, waits for them, and re-layouts  26.6 us
    all_to_all x2, starting transfers between devices, return_rows(): lax.all_to_all(jnp.stack([shares] * lax.axis_size('fsdp')), 'fsdp', 0, 0)  24.8 us
  transfers between devices with their start and end apart: 22, of which 10 were waited for; matrix products, arithmetic and copies ran while one was open for 10% of the time, Pallas kernels for 0%

profile of v1, /device:TPU:6, one launch (start us, length us, event | category | flops | bytes accessed | tf_op | source)
XLA Modules:
  0.0 510.7 jit_solution(2699267608159276541)
XLA Ops:
  7.0 6.6 %all-to-all-start = ((bf16[8,48,3072]{2,1,0:T(8,128)(2,1)}), bf16[8,48,3072]{2,1,0:T(8,128)(2,1)}, u32[]{:S(2)}, u32[]{:S(2)}) async-start(bf16[8,48,3072]{2,1,0:T(8,128)(2,1)} %bitcast.78), calls=%async_computation | async-start | bytes 4718592 | tf_op jit(solution)/shard_map/all_to_all | solution.py:27
  17.1 25.5 %all-to-all-done = bf16[8,48,3072]{2,1,0:T(8,128)(2,1)} async-done(((bf16[8,48,3072]{2,1,0:T(8,128)(2,1)}), bf16[8,48,3072]{2,1,0:T(8,128)(2,1)}, u32[]{:S(2)}, u32[]{:S(2)}) %all-to-all-start) | async-done | bytes 2359328 | tf_op jit(solution)/shard_map/all_to_all | solution.py:27
  42.6 5.4 %all-to-all-start.3 = ((bf16[8,48,3072]{2,1,0:T(8,128)(2,1)}), bf16[8,48,3072]{2,1,0:T(8,128)(2,1)}, u32[]{:S(2)}, u32[]{:S(2)}) async-start(bf16[8,48,3072]{2,1,0:T(8,128)(2,1)} %bitcast.79), calls=%async_computation.3 | async-start | bytes 4718592 | tf_op jit(solution)/shard_map/all_to_all | solution.py:27
  54.9 21.9 %all-to-all-done.3 = bf16[8,48,3072]{2,1,0:T(8,128)(2,1)} async-done(((bf16[8,48,3072]{2,1,0:T(8,128)(2,1)}), bf16[8,48,3072]{2,1,0:T(8,128)(2,1)}, u32[]{:S(2)}, u32[]{:S(2)}) %all-to-all-start.3) | async-done | bytes 2359328 | tf_op jit(solution)/shard_map/all_to_all | solution.py:27
  84.8 86.0 %fusion.34 = (bf16[16,3072]{1,0:T(8,128)(2,1)S(1)}, bf16[16,3072]{1,0:T(8,128)(2,1)S(1)}) fusion(bf16[384,3072]{1,0:T(8,128)(2,1)S(1)} %copy-done.4, bf16[384,3072]{1,0:T(8,128)(2,1)} %add_convert_fusion), kind=kCustom, calls=%all-reduce-scatter.2 | all-reduce-scatter fusion | flops 3145729 | bytes 4916224
  176.1 10.9 %collective-permute-start.3 = (bf16[16,3072]{1,0:T(8,128)(2,1)S(1)}, bf16[16,3072]{1,0:T(8,128)(2,1)S(1)}, u32[]{:S(2)}, u32[]{:S(2)}) collective-permute-start(bf16[16,3072]{1,0:T(8,128)(2,1)S(1)} %get-tuple-element.10), channel_id=1, source_target_pairs={{0,4},{1,5},{2,6},{3,7},{4,8},{5,9},{6,10},{7,11},{8,12},{9,13},{1... | collective-permute-start | bytes 294920
  191.5 4.7 collective-permute-start.6
  197.5 5.2 %collective-permute-done.5 = bf16[16,3072]{1,0:T(8,128)(2,1)S(1)} collective-permute-done((bf16[16,3072]{1,0:T(8,128)(2,1)S(1)}, bf16[16,3072]{1,0:T(8,128)(2,1)S(1)}, u32[]{:S(2)}, u32[]{:S(2)}) %collective-permute-start.5) | collective-permute-done | bytes 98336
  202.6 4.9 collective-permute-done.6
  211.7 8.4 %all-to-all-start.1 = ((bf16[32,12,3072]{2,1,0:T(8,128)(2,1)}), bf16[32,12,3072]{2,1,0:T(8,128)(2,1)S(1)}, u32[]{:S(2)}, u32[]{:S(2)}) async-start(bf16[32,12,3072]{2,1,0:T(8,128)(2,1)} %stack.10), calls=%async_computation.1 | async-start | bytes 6291456 | tf_op jit(solution)/shard_map/all_to_all | solution.py:39
  223.6 4.3 collective-permute-start.11
  227.9 4.6 collective-permute-start.15
  232.5 6.1 %collective-permute-start.12 = (bf16[16,3072]{1,0:T(8,128)(2,1)S(1)}, bf16[16,3072]{1,0:T(8,128)(2,1)S(1)}, u32[]{:S(2)}, u32[]{:S(2)}) collective-permute-start(bf16[16,3072]{1,0:T(8,128)(2,1)S(1)} %get-tuple-element.11), channel_id=1, source_target_pairs={{0,5},{1,6},{2,7},{3,8},{4,9},{5,10},{6,11},{7,12},{8,13},{9,14},{... | collective-permute-start | bytes 294920
  238.6 5.5 %collective-permute-start.13 = (bf16[16,3072]{1,0:T(8,128)(2,1)S(1)}, bf16[16,3072]{1,0:T(8,128)(2,1)S(1)}, u32[]{:S(2)}, u32[]{:S(2)}) collective-permute-start(bf16[16,3072]{1,0:T(8,128)(2,1)S(1)} %get-tuple-element.11), channel_id=1, source_target_pairs={{0,6},{1,7},{2,8},{3,9},{4,10},{5,11},{6,12},{7,13},{8,14},{9,15},... | collective-permute-start | bytes 294920
  244.2 57.2 %collective-permute-done.15 = bf16[12,3072]{1,0:T(8,128)(2,1)S(1)} collective-permute-done((bf16[12,3072]{1,0:T(8,128)(2,1)S(1)}, bf16[12,3072]{1,0:T(8,128)(2,1)S(1)}, u32[]{:S(2)}, u32[]{:S(2)}) %collective-permute-start.15) | collective-permute-done | bytes 73760
  302.7 10.4 %collective-permute-start.8 = (bf16[16,3072]{1,0:T(8,128)(2,1)S(1)}, bf16[16,3072]{1,0:T(8,128)(2,1)S(1)}, u32[]{:S(2)}, u32[]{:S(2)}) collective-permute-start(bf16[16,3072]{1,0:T(8,128)(2,1)S(1)} %get-tuple-element.11), channel_id=1, source_target_pairs={{0,1},{1,2},{2,3},{3,4},{4,5},{5,6},{6,7},{7,8},{8,9},{9,10},{10,1... | collective-permute-start | bytes 294920
  317.6 20.6 %concatenate.1 = bf16[140,3072]{1,0:T(8,128)(2,1)} concatenate(bf16[12,3072]{1,0:T(8,128)(2,1)} %copy-done.15, bf16[16,3072]{1,0:T(8,128)(2,1)} %copy-done.18, bf16[16,3072]{1,0:T(8,128)(2,1)} %copy-done.17, bf16[16,3072]{1,0:T(8,128)(2,1)} %copy-done.16, bf16[16,3072]{1,0:T(8,128)(2,1)} %copy-done.14, bf16[16,3072]{1,0:T(8,128)(2,1)S(1)} %collective-permute-done.10, ...), dimensions={0} | concatenate | bytes 1720320
  341.3 16.4 %all-to-all-start.4 = ((bf16[32,12,3072]{2,1,0:T(8,128)(2,1)}), bf16[32,12,3072]{2,1,0:T(8,128)(2,1)}, u32[]{:S(2)}, u32[]{:S(2)}) async-start(bf16[32,12,3072]{2,1,0:T(8,128)(2,1)} %stack.11), calls=%async_computation.4 | async-start | bytes 6291456 | tf_op jit(solution)/shard_map/all_to_all | solution.py:39
  359.8 72.1 %all-to-all-done.4 = bf16[32,12,3072]{2,1,0:T(8,128)(2,1)} async-done(((bf16[32,12,3072]{2,1,0:T(8,128)(2,1)}), bf16[32,12,3072]{2,1,0:T(8,128)(2,1)}, u32[]{:S(2)}, u32[]{:S(2)}) %all-to-all-start.4) | async-done | bytes 2359328 | tf_op jit(solution)/shard_map/all_to_all | solution.py:39
  431.8 5.9 %all-to-all-start.2 = ((bf16[8,48,3072]{2,1,0:T(8,128)(2,1)}), bf16[8,48,3072]{2,1,0:T(8,128)(2,1)S(1)}, u32[]{:S(2)}, u32[]{:S(2)}) async-start(bf16[8,48,3072]{2,1,0:T(8,128)(2,1)} %reshape_reshape.6), calls=%async_computation.2 | async-start | bytes 4718592 | tf_op jit(solution)/shard_map/all_to_all | solution.py:41
  437.8 4.2 reshape_reshape.7
  442.0 28.2 %all-to-all-done.2 = bf16[8,48,3072]{2,1,0:T(8,128)(2,1)S(1)} async-done(((bf16[8,48,3072]{2,1,0:T(8,128)(2,1)}), bf16[8,48,3072]{2,1,0:T(8,128)(2,1)S(1)}, u32[]{:S(2)}, u32[]{:S(2)}) %all-to-all-start.2) | async-done | bytes 2359328 | tf_op jit(solution)/shard_map/all_to_all | solution.py:41
  470.3 5.4 %all-to-all-start.5 = ((bf16[8,48,3072]{2,1,0:T(8,128)(2,1)}), bf16[8,48,3072]{2,1,0:T(8,128)(2,1)}, u32[]{:S(2)}, u32[]{:S(2)}) async-start(bf16[8,48,3072]{2,1,0:T(8,128)(2,1)} %reshape_reshape.7), calls=%async_computation.5 | async-start | bytes 4718592 | tf_op jit(solution)/shard_map/all_to_all | solution.py:41
  489.1 13.5 %all-to-all-done.5 = bf16[8,48,3072]{2,1,0:T(8,128)(2,1)} async-done(((bf16[8,48,3072]{2,1,0:T(8,128)(2,1)}), bf16[8,48,3072]{2,1,0:T(8,128)(2,1)}, u32[]{:S(2)}, u32[]{:S(2)}) %all-to-all-start.5) | async-done | bytes 2359328 | tf_op jit(solution)/shard_map/all_to_all | solution.py:41
  (109 shorter events, 74.9 us)
Async XLA Ops:
  0.6 76.2 %copy-start = (bf16[1,256,3072]{2,1,0:T(8,128)(2,1)S(1)}, bf16[1,256,3072]{2,1,0:T(8,128)(2,1)}, u32[]{:S(2)}) copy-start(bf16[1,256,3072]{2,1,0:T(8,128)(2,1)} %param.13) | copy-start | bytes 4718596
  7.0 35.5 %all-to-all-start = ((bf16[8,48,3072]{2,1,0:T(8,128)(2,1)}), bf16[8,48,3072]{2,1,0:T(8,128)(2,1)}, u32[]{:S(2)}, u32[]{:S(2)}) async-start(bf16[8,48,3072]{2,1,0:T(8,128)(2,1)} %bitcast.78), calls=%async_computation | async-start | bytes 4718592 | tf_op jit(solution)/shard_map/all_to_all | solution.py:27
  42.6 34.2 %all-to-all-start.3 = ((bf16[8,48,3072]{2,1,0:T(8,128)(2,1)}), bf16[8,48,3072]{2,1,0:T(8,128)(2,1)}, u32[]{:S(2)}, u32[]{:S(2)}) async-start(bf16[8,48,3072]{2,1,0:T(8,128)(2,1)} %bitcast.79), calls=%async_computation.3 | async-start | bytes 4718592 | tf_op jit(solution)/shard_map/all_to_all | solution.py:27
  84.8 111.4 %copy-start.21 = (u32[256]{0:T(256)S(1)}, u32[256]{0:T(256)}, u32[]{:S(2)}) copy-start(u32[256]{0:T(256)} %constant.17) | copy-start | bytes 3076
  170.9 17.8 %collective-permute-start = (bf16[16,3072]{1,0:T(8,128)(2,1)S(1)}, bf16[16,3072]{1,0:T(8,128)(2,1)S(1)}, u32[]{:S(2)}, u32[]{:S(2)}) collective-permute-start(bf16[16,3072]{1,0:T(8,128)(2,1)S(1)} %get-tuple-element.10), channel_id=1, source_target_pairs={{0,1},{1,2},{2,3},{3,4},{4,5},{5,6},{6,7},{7,8},{8,9},{9,10},{10,1... | collective-permute-start | bytes 294920
  172.2 19.3 %collective-permute-start.1 = (bf16[16,3072]{1,0:T(8,128)(2,1)S(1)}, bf16[16,3072]{1,0:T(8,128)(2,1)S(1)}, u32[]{:S(2)}, u32[]{:S(2)}) collective-permute-start(bf16[16,3072]{1,0:T(8,128)(2,1)S(1)} %get-tuple-element.10), channel_id=1, source_target_pairs={{0,2},{1,3},{2,4},{3,5},{4,6},{5,7},{6,8},{7,9},{8,10},{9,11},{10,... | collective-permute-start | bytes 294920
  173.5 13.5 %collective-permute-start.7 = (bf16[12,3072]{1,0:T(8,128)(2,1)S(1)}, bf16[12,3072]{1,0:T(8,128)(2,1)S(1)}, u32[]{:S(2)}, u32[]{:S(2)}) collective-permute-start(bf16[12,3072]{1,0:T(8,128)(2,1)S(1)} %slice.35), channel_id=1, source_target_pairs={{0,8},{1,9},{2,10},{3,11},{4,12},{5,13},{6,14},{7,15},{8,16},{9,17... | collective-permute-start | bytes 221192
  174.8 22.6 %collective-permute-start.2 = (bf16[16,3072]{1,0:T(8,128)(2,1)S(1)}, bf16[16,3072]{1,0:T(8,128)(2,1)S(1)}, u32[]{:S(2)}, u32[]{:S(2)}) collective-permute-start(bf16[16,3072]{1,0:T(8,128)(2,1)S(1)} %get-tuple-element.10), channel_id=1, source_target_pairs={{0,3},{1,4},{2,5},{3,6},{4,7},{5,8},{6,9},{7,10},{8,11},{9,12},{10... | collective-permute-start | bytes 294920
  176.1 21.3 %collective-permute-start.3 = (bf16[16,3072]{1,0:T(8,128)(2,1)S(1)}, bf16[16,3072]{1,0:T(8,128)(2,1)S(1)}, u32[]{:S(2)}, u32[]{:S(2)}) collective-permute-start(bf16[16,3072]{1,0:T(8,128)(2,1)S(1)} %get-tuple-element.10), channel_id=1, source_target_pairs={{0,4},{1,5},{2,6},{3,7},{4,8},{5,9},{6,10},{7,11},{8,12},{9,13},{1... | collective-permute-start | bytes 294920
  187.0 10.4 %collective-permute-start.4 = (bf16[16,3072]{1,0:T(8,128)(2,1)S(1)}, bf16[16,3072]{1,0:T(8,128)(2,1)S(1)}, u32[]{:S(2)}, u32[]{:S(2)}) collective-permute-start(bf16[16,3072]{1,0:T(8,128)(2,1)S(1)} %get-tuple-element.10), channel_id=1, source_target_pairs={{0,5},{1,6},{2,7},{3,8},{4,9},{5,10},{6,11},{7,12},{8,13},{9,14},{... | collective-permute-start | bytes 294920
  188.7 13.9 %collective-permute-start.5 = (bf16[16,3072]{1,0:T(8,128)(2,1)S(1)}, bf16[16,3072]{1,0:T(8,128)(2,1)S(1)}, u32[]{:S(2)}, u32[]{:S(2)}) collective-permute-start(bf16[16,3072]{1,0:T(8,128)(2,1)S(1)} %get-tuple-element.10), channel_id=1, source_target_pairs={{0,6},{1,7},{2,8},{3,9},{4,10},{5,11},{6,12},{7,13},{8,14},{9,15},... | collective-permute-start | bytes 294920
  191.5 16.1 %collective-permute-start.6 = (bf16[16,3072]{1,0:T(8,128)(2,1)S(1)}, bf16[16,3072]{1,0:T(8,128)(2,1)S(1)}, u32[]{:S(2)}, u32[]{:S(2)}) collective-permute-start(bf16[16,3072]{1,0:T(8,128)(2,1)S(1)} %get-tuple-element.10), channel_id=1, source_target_pairs={{0,7},{1,8},{2,9},{3,10},{4,11},{5,12},{6,13},{7,14},{8,15},{9,16}... | collective-permute-start | bytes 294920
  211.7 127.4 %all-to-all-start.1 = ((bf16[32,12,3072]{2,1,0:T(8,128)(2,1)}), bf16[32,12,3072]{2,1,0:T(8,128)(2,1)S(1)}, u32[]{:S(2)}, u32[]{:S(2)}) async-start(bf16[32,12,3072]{2,1,0:T(8,128)(2,1)} %stack.10), calls=%async_computation.1 | async-start | bytes 6291456 | tf_op jit(solution)/shard_map/all_to_all | solution.py:39
  220.2 82.5 %collective-permute-start.10 = (bf16[16,3072]{1,0:T(8,128)(2,1)S(1)}, bf16[16,3072]{1,0:T(8,128)(2,1)S(1)}, u32[]{:S(2)}, u32[]{:S(2)}) collective-permute-start(bf16[16,3072]{1,0:T(8,128)(2,1)S(1)} %get-tuple-element.11), channel_id=1, source_target_pairs={{0,3},{1,4},{2,5},{3,6},{4,7},{5,8},{6,9},{7,10},{8,11},{9,12},{10... | collective-permute-start | bytes 294920
  223.6 89.5 %collective-permute-start.11 = (bf16[16,3072]{1,0:T(8,128)(2,1)S(1)}, bf16[16,3072]{1,0:T(8,128)(2,1)S(1)}, u32[]{:S(2)}, u32[]{:S(2)}) collective-permute-start(bf16[16,3072]{1,0:T(8,128)(2,1)S(1)} %get-tuple-element.11), channel_id=1, source_target_pairs={{0,4},{1,5},{2,6},{3,7},{4,8},{5,9},{6,10},{7,11},{8,12},{9,13},{1... | collective-permute-start | bytes 294920
  227.9 73.5 %collective-permute-start.15 = (bf16[12,3072]{1,0:T(8,128)(2,1)S(1)}, bf16[12,3072]{1,0:T(8,128)(2,1)S(1)}, u32[]{:S(2)}, u32[]{:S(2)}) collective-permute-start(bf16[12,3072]{1,0:T(8,128)(2,1)S(1)} %slice.36), channel_id=1, source_target_pairs={{0,8},{1,9},{2,10},{3,11},{4,12},{5,13},{6,14},{7,15},{8,16},{9,17... | collective-permute-start | bytes 221192
  232.5 82.6 %collective-permute-start.12 = (bf16[16,3072]{1,0:T(8,128)(2,1)S(1)}, bf16[16,3072]{1,0:T(8,128)(2,1)S(1)}, u32[]{:S(2)}, u32[]{:S(2)}) collective-permute-start(bf16[16,3072]{1,0:T(8,128)(2,1)S(1)} %get-tuple-element.11), channel_id=1, source_target_pairs={{0,5},{1,6},{2,7},{3,8},{4,9},{5,10},{6,11},{7,12},{8,13},{9,14},{... | collective-permute-start | bytes 294920
  238.6 76.5 %collective-permute-start.13 = (bf16[16,3072]{1,0:T(8,128)(2,1)S(1)}, bf16[16,3072]{1,0:T(8,128)(2,1)S(1)}, u32[]{:S(2)}, u32[]{:S(2)}) collective-permute-start(bf16[16,3072]{1,0:T(8,128)(2,1)S(1)} %get-tuple-element.11), channel_id=1, source_target_pairs={{0,6},{1,7},{2,8},{3,9},{4,10},{5,11},{6,12},{7,13},{8,14},{9,15},... | collective-permute-start | bytes 294920
  301.4 13.9 %collective-permute-start.14 = (bf16[16,3072]{1,0:T(8,128)(2,1)S(1)}, bf16[16,3072]{1,0:T(8,128)(2,1)S(1)}, u32[]{:S(2)}, u32[]{:S(2)}) collective-permute-start(bf16[16,3072]{1,0:T(8,128)(2,1)S(1)} %get-tuple-element.11), channel_id=1, source_target_pairs={{0,7},{1,8},{2,9},{3,10},{4,11},{5,12},{6,13},{7,14},{8,15},{9,16}... | collective-permute-start | bytes 294920
  302.7 12.6 %collective-permute-start.8 = (bf16[16,3072]{1,0:T(8,128)(2,1)S(1)}, bf16[16,3072]{1,0:T(8,128)(2,1)S(1)}, u32[]{:S(2)}, u32[]{:S(2)}) collective-permute-start(bf16[16,3072]{1,0:T(8,128)(2,1)S(1)} %get-tuple-element.11), channel_id=1, source_target_pairs={{0,1},{1,2},{2,3},{3,4},{4,5},{5,6},{6,7},{7,8},{8,9},{9,10},{10,1... | collective-permute-start | bytes 294920
  313.1 4.5 collective-permute-start.9
  341.3 90.6 %all-to-all-start.4 = ((bf16[32,12,3072]{2,1,0:T(8,128)(2,1)}), bf16[32,12,3072]{2,1,0:T(8,128)(2,1)}, u32[]{:S(2)}, u32[]{:S(2)}) async-start(bf16[32,12,3072]{2,1,0:T(8,128)(2,1)} %stack.11), calls=%async_computation.4 | async-start | bytes 6291456 | tf_op jit(solution)/shard_map/all_to_all | solution.py:39
  431.8 38.4 %all-to-all-start.2 = ((bf16[8,48,3072]{2,1,0:T(8,128)(2,1)}), bf16[8,48,3072]{2,1,0:T(8,128)(2,1)S(1)}, u32[]{:S(2)}, u32[]{:S(2)}) async-start(bf16[8,48,3072]{2,1,0:T(8,128)(2,1)} %reshape_reshape.6), calls=%async_computation.2 | async-start | bytes 4718592 | tf_op jit(solution)/shard_map/all_to_all | solution.py:41
  470.3 32.3 %all-to-all-start.5 = ((bf16[8,48,3072]{2,1,0:T(8,128)(2,1)}), bf16[8,48,3072]{2,1,0:T(8,128)(2,1)}, u32[]{:S(2)}, u32[]{:S(2)}) async-start(bf16[8,48,3072]{2,1,0:T(8,128)(2,1)} %reshape_reshape.7), calls=%async_computation.5 | async-start | bytes 4718592 | tf_op jit(solution)/shard_map/all_to_all | solution.py:41
  (20 other events, 81.4 us)
